TPU v7x, 32 devices: a whole 2x2x4 slice. The times are simulated.
32 devices in a mesh: parts: 2 (over y), seq: 16 (over z, x, core).
Axes of the slice: x: 2, y: 2, z: 4, core: 2. Of those that a mesh axis runs over, the one named last changes fastest.
Arguments:
- queries: float32 [4096, 4096], P(('parts', 'seq')), parts along dimension 0, may hold values from -11 to 11
- visual_keys: float32 [4096, 512], P(('parts', 'seq')), parts along dimension 0, may hold values from -4 to 4
- visual_value_rows: float32 [4096, 512], P(('parts', 'seq')), parts along dimension 0, may hold values from -6 to 6
- output_gradient: float32 [4096, 4096], P(('parts', 'seq')), parts along dimension 0, may hold values from -6 to 6
- query_head_gate: float32 [32], replicated, may hold values from 0.3 to 2
- window_lists: int32 [2, 6], P('parts'), parts along dimension 0, may hold values from 0 to 15, as said below
- block_place: int32 [32], P('parts'), parts along dimension 0, may hold values from 0 to 15, each once
Outputs:
- output: float32 [4096, 4096], P(('parts', 'seq')), parts along dimension 0
- grad_queries: float32 [4096, 4096], P(('parts', 'seq')), parts along dimension 0
- grad_keys: float32 [4096, 512], P(('parts', 'seq')), parts along dimension 0
- grad_values: float32 [4096, 512], P(('parts', 'seq')), parts along dimension 0
There are 2 independent parts, one for each index of `parts`. A program takes and returns all parts, laid end to end along the dimension named above; an argument that names none is the same for every part. Nothing has to cross between parts.
Inputs may be any that keep to these rules, and one draw needn't show every extreme that they name: `window_lists`: each row names 6 different visual blocks.
All inputs are finite; a program needn't handle non-finite values.
Results may differ from a plain program's by a relative error of at most 0.0003.
Values sent between devices are 32-bit elements; how exact they have to be, the bound alone decides.
A program may use at most 128 MiB of HBM per device.

v0:
```python
import functools
import math

import jax
import jax.numpy as jnp
from jax import lax
from jax.experimental import pallas as pl
from jax.experimental.pallas import tpu as pltpu
from jax.sharding import PartitionSpec as P

HEAD_FEATURES = 128
BLOCK_TOKENS = 128
WINDOW_ROWS = 2048
HIGHEST = lax.Precision.HIGHEST
MESH = pl.DeviceIdType.MESH
D = HEAD_FEATURES
HEADS_PER_STEP = 4


def split(x):
    hi = x.astype(jnp.bfloat16)
    return hi, (x - hi.astype(jnp.float32)).astype(jnp.bfloat16)


def dot(a, b):
    return jnp.dot(a, b, preferred_element_type=jnp.float32)


def load_head(k, v, kcat, vcat, kt2, vt2):
    kh, kl = split(k)
    kcat[...] = jnp.concatenate([kh, kl, kh], axis=1)
    vh, vl = split(v)
    vcat[...] = jnp.concatenate([vh, vl, vh], axis=1)
    th, tl = split(k.T)
    kt2[...] = jnp.concatenate([th, tl], axis=0)
    th, tl = split(v.T)
    vt2[...] = jnp.concatenate([th, tl], axis=0)


def heads_down(x):
    return jnp.concatenate([x[:, i : i + D] for i in range(0, x.shape[1], D)], axis=0)


def heads_across(x, rows):
    return jnp.concatenate([x[:, i : i + rows].T for i in range(0, x.shape[1], rows)], axis=1)


def attend_step(q, g, gate, kcat, vcat, kt2, vt2):
    inverse_root = D ** (-0.5)
    rows = q.shape[0]
    qr = heads_down(q) * inverse_root
    qt = qr.T
    th, tl = split(qt * math.log2(math.e))
    scores = dot(kcat[...], jnp.concatenate([th, th, tl], axis=0))
    row_max = jnp.max(scores, axis=0, keepdims=True)
    raised = jnp.exp2(scores - row_max)
    total = jnp.sum(raised, axis=0, keepdims=True)
    inv = 1.0 / total
    eh, el = split(raised)
    o2 = dot(vt2[...], eh)
    att = (o2[:D] + o2[D:] + dot(vt2[:D], el)) * inv
    out = heads_across(att, rows) * gate
    gt = heads_down(g * gate).T
    row_dot = jnp.sum(gt * att, axis=0, keepdims=True) * inv
    gt = gt * inv
    th, tl = split(gt)
    gw = dot(vcat[...], jnp.concatenate([th, th, tl], axis=0))
    ds = raised * (gw - row_dot)
    dh, dl = split(ds)
    q2 = dot(kt2[...], dh)
    gq = (q2[:D] + q2[D:] + dot(kt2[:D], dl)) * inverse_root
    gq = heads_across(gq, rows)
    gh, gl = split(gt.T)
    v2 = dot(eh, jnp.concatenate([gh, gl], axis=1))
    gv = v2[:, :D] + v2[:, D:] + dot(el, gh)
    qh, ql = split(qr)
    k2 = dot(dh, jnp.concatenate([qh, ql], axis=1))
    gk = k2[:, :D] + k2[:, D:] + dot(dl, qh)
    return out, gq, gk, gv


def attend_kernel(q_ref, g_ref, gate_ref, k_ref, v_ref, out_ref, gq_ref, gk_ref, gv_ref, kcat, vcat, kt2, vt2):
    first = pl.program_id(1) == 0

    @pl.when(first)
    def _():
        load_head(k_ref[...], v_ref[...], kcat, vcat, kt2, vt2)

    out, gq, gk, gv = attend_step(q_ref[...], g_ref[...], gate_ref[...], kcat, vcat, kt2, vt2)
    out_ref[...] = out
    gq_ref[...] = gq

    @pl.when(first)
    def _():
        gk_ref[...] = gk
        gv_ref[...] = gv

    @pl.when(jnp.logical_not(first))
    def _():
        gk_ref[...] += gk
        gv_ref[...] += gv


def attend(q, g, gate_row, k, v):
    rows, width = q.shape
    keys, kv_width = k.shape
    key_heads = kv_width // D
    wide = HEADS_PER_STEP * D
    steps = width // key_heads // wide
    big = pl.BlockSpec((rows, wide), lambda h, s: (0, h * steps + s))
    gate = pl.BlockSpec((1, wide), lambda h, s: (0, h * steps + s))
    kv = pl.BlockSpec((keys, D), lambda h, s: (0, h))
    f32 = jnp.float32
    return pl.pallas_call(
        attend_kernel,
        grid=(key_heads, steps),
        in_specs=[big, big, gate, kv, kv],
        out_specs=[big, big, kv, kv],
        out_shape=[
            jax.ShapeDtypeStruct(q.shape, f32),
            jax.ShapeDtypeStruct(q.shape, f32),
            jax.ShapeDtypeStruct(k.shape, f32),
            jax.ShapeDtypeStruct(k.shape, f32),
        ],
        scratch_shapes=[
            pltpu.VMEM((keys, 3 * D), jnp.bfloat16),
            pltpu.VMEM((keys, 3 * D), jnp.bfloat16),
            pltpu.VMEM((2 * D, keys), jnp.bfloat16),
            pltpu.VMEM((2 * D, keys), jnp.bfloat16),
        ],
        compiler_params=pltpu.CompilerParams(
            dimension_semantics=("arbitrary", "arbitrary"), vmem_limit_bytes=60 * 1024 * 1024
        ),
    )(q, g, gate_row, k, v)


def gate_row_of(query_head_gate):
    return jnp.repeat(jnp.tanh(query_head_gate), D)[None, :]


def local(
    queries,
    visual_keys,
    visual_value_rows,
    output_gradient,
    query_head_gate,
    window_lists,
    block_place,
):
    row_count = queries.shape[0]
    feature_width = visual_keys.shape[1]
    list_len = window_lists.shape[1]
    devices = lax.axis_size("seq")
    window_devices = WINDOW_ROWS // row_count
    blocks_here = visual_keys.shape[0] // BLOCK_TOKENS
    piece_len = BLOCK_TOKENS // devices
    channels = 2 * feature_width
    positions = devices * blocks_here
    stacked = jnp.concatenate([visual_keys, visual_value_rows], axis=1)
    stacked = stacked.reshape(blocks_here, devices, piece_len, channels)
    spread = lax.all_to_all(stacked, "seq", split_axis=1, concat_axis=0, tiled=True).reshape(
        positions, piece_len, channels
    )
    target_window = jnp.arange(devices, dtype=jnp.int32) // window_devices
    wanted = jnp.take(block_place, jnp.take(window_lists, target_window, axis=0), axis=0)
    fetched = lax.all_to_all(spread[wanted], "seq", split_axis=0, concat_axis=2, tiled=True)
    fetched = fetched.reshape(list_len * BLOCK_TOKENS, channels)
    output, grad_query, grad_key, grad_value = attend(
        queries,
        output_gradient,
        gate_row_of(query_head_gate),
        fetched[:, :feature_width],
        fetched[:, feature_width:],
    )
    gradients = jnp.concatenate([grad_key, grad_value], axis=1)
    collected = lax.all_to_all(
        gradients.reshape(list_len, devices, piece_len, channels),
        "seq",
        split_axis=1,
        concat_axis=1,
        tiled=True,
    )
    onehot = (wanted.T.reshape(1, -1) == jnp.arange(positions, dtype=jnp.int32)[:, None]).astype(
        jnp.float32
    )
    summed = jnp.dot(
        onehot,
        collected.reshape(list_len * devices, piece_len * channels),
        precision=HIGHEST,
        preferred_element_type=jnp.float32,
    )
    returned = lax.all_to_all(
        summed.reshape(devices, blocks_here, piece_len, channels),
        "seq",
        split_axis=0,
        concat_axis=2,
        tiled=True,
    )
    returned = returned.reshape(blocks_here * BLOCK_TOKENS, channels)
    return (output, grad_query, returned[:, :feature_width], returned[:, feature_width:])


def solution(mesh):
    rows = P(("parts", "seq"), None)
    return jax.shard_map(
        local,
        mesh=mesh,
        in_specs=(rows, rows, rows, rows, P(), P("parts", None), P("parts")),
        out_specs=(rows, rows, rows, rows),
        check_vma=False,
    )
```

profile of v0, /device:TPU:0, one launch (start us, length us, event | category | flops | bytes accessed | tf_op | source)
XLA Modules:
  0.0 233.2 jit_solution(411532552848303589)
XLA Ops:
  0.6 0.0 copy-start
  0.6 1.9 maximum_bitcast_fusion
  2.5 7.4 %all-to-all-start = ((f32[1,16,8,1024]{3,2,0,1:T(8,128)}), f32[1,16,8,1024]{3,2,0,1:T(8,128)S(1)}, u32[]{:S(2)}, u32[]{:S(2)}) async-start(f32[1,16,8,1024]{3,2,0,1:T(8,128)} %maximum_bitcast_fusion), calls=%async_computation | async-start | bytes 1048576 | tf_op jit(solution)/shard_map/all_to_all | solution.py:161
  9.9 0.7 compare_select_fusion.2
  10.7 0.1 reshape.199
  10.8 0.0 copy-done
  10.8 0.0 copy-start.1
  10.8 1.2 gather_fusion
  12.0 0.1 gather.20
  12.1 0.0 copy-done.1
  12.1 0.1 compare_select_fusion.1
  12.2 0.1 reshape.207
  12.3 11.9 %all-to-all-done = f32[1,16,8,1024]{3,2,0,1:T(8,128)S(1)} async-done(((f32[1,16,8,1024]{3,2,0,1:T(8,128)}), f32[1,16,8,1024]{3,2,0,1:T(8,128)S(1)}, u32[]{:S(2)}, u32[]{:S(2)}) %all-to-all-start) | async-done | bytes 524320 | tf_op jit(solution)/shard_map/all_to_all | solution.py:161
  24.2 2.4 %gather_fusion.1 = f32[96,8,1024]{2,1,0:T(8,128)} fusion(f32[16,8,1024]{2,1,0:T(8,128)S(1)} %bitcast.49, s32[1024]{0:T(1024)S(1)} %pad_clamp_fusion), kind=kCustom, calls=%fused_computation.1 | custom fusion | bytes 6291840 | tf_op jit(solution)/shard_map/gather | solution.py:166
  26.6 0.0 copy-start.2
  26.6 4.3 %all-to-all-start.1 = ((f32[16,6,8,1024]{3,2,1,0:T(8,128)}), f32[16,6,8,1024]{3,2,1,0:T(8,128)S(1)}, u32[]{:S(2)}, u32[]{:S(2)}) async-start(f32[16,6,8,1024]{3,2,1,0:T(8,128)} %bitcast.51), calls=%async_computation.1 | async-start | bytes 6291456 | tf_op jit(solution)/shard_map/all_to_all | solution.py:166
  30.9 0.0 copy-done.2
  30.9 59.2 %all-to-all-done.1 = f32[16,6,8,1024]{3,2,1,0:T(8,128)S(1)} async-done(((f32[16,6,8,1024]{3,2,1,0:T(8,128)}), f32[16,6,8,1024]{3,2,1,0:T(8,128)S(1)}, u32[]{:S(2)}, u32[]{:S(2)}) %all-to-all-start.1) | async-done | bytes 3145760 | tf_op jit(solution)/shard_map/all_to_all | solution.py:166
  90.1 0.2 copy.21
  90.3 1.9 fusion.12
  92.3 0.7 broadcast_in_dim.25
  92.9 27.7 %shard_map.102 = (f32[128,4096]{1,0:T(8,128)}, f32[128,4096]{1,0:T(8,128)}, f32[768,512]{1,0:T(8,128)}, f32[768,512]{1,0:T(8,128)}) custom-call(f32[128,4096]{1,0:T(8,128)} %q_ref.1, f32[128,4096]{1,0:T(8,128)} %g_ref.1, f32[1,4096]{1,0:T(1,128)} %bitcast.56, f32[768,512]{1,0:T(8,128)} %get-tuple-element.13.k_ref, f32[768,512]{1,0:T(8,128)} %get-tuple-element.12.v_ref), custom_call_target="tpu_custom_call" | custom-call | tf_op jit(solution)/shard_map/pallas_call | solution.py:114
  120.6 2.2 pad_maximum_fusion
  122.8 2.0 copy.23
  124.8 15.4 %all-to-all-start.2 = ((f32[6,16,8,1024]{3,2,0,1:T(8,128)}), f32[6,16,8,1024]{3,2,0,1:T(8,128)S(1)}, u32[]{:S(2)}, u32[]{:S(2)}) async-start(f32[6,16,8,1024]{3,2,0,1:T(8,128)} %copy.23), calls=%async_computation.2 | async-start | bytes 6291456 | tf_op jit(solution)/shard_map/all_to_all | solution.py:176
  140.3 0.1 reshape.198
  140.3 0.1 bitcast_select_fusion
  140.4 0.1 copy.22
  140.5 0.1 eq.15
  140.6 58.9 %all-to-all-done.2 = f32[6,16,8,1024]{3,2,0,1:T(8,128)S(1)} async-done(((f32[6,16,8,1024]{3,2,0,1:T(8,128)}), f32[6,16,8,1024]{3,2,0,1:T(8,128)S(1)}, u32[]{:S(2)}, u32[]{:S(2)}) %all-to-all-start.2) | async-done | bytes 3145760 | tf_op jit(solution)/shard_map/all_to_all | solution.py:176
  199.5 0.2 copy.24
  199.7 2.9 %fusion.3 = f32[16,1,8,1024]{3,0,2,1:T(8,128)S(1)} fusion(s32[96]{0:T(128)S(1)} %eq.15, f32[12,8,8,1024]{3,2,1,0:T(8,128)S(1)} %bitcast.54), kind=kOutput, calls=%fused_computation.6 | convolution fusion | flops 150996480 | bytes 3670400 | tf_op jit(solution)/shard_map/dot_general | solution.py:186
  202.6 0.3 copy.26
  202.9 29.5 %all_to_all.38 = f32[16,1,8,1024]{3,2,1,0:T(8,128)S(1)} all-to-all(f32[16,1,8,1024]{3,2,1,0:T(8,128)S(1)} %copy.26), channel_id=1, replica_groups=mesh['parts'=2,'seq'=16] {'seq'}, dimensions={0} | all-to-all | bytes 1048576 | tf_op jit(solution)/shard_map/all_to_all | solution.py:192
  232.4 0.8 fusion.13
  (4 shorter events, 0.0 us)
Async XLA Ops:
  0.6 10.1 %copy-start = (s32[16]{0:T(128)S(1)}, s32[16]{0:T(128)}, u32[]{:S(2)}) copy-start(s32[16]{0:T(128)} %param.13) | copy-start | bytes 196
  2.5 21.7 %all-to-all-start = ((f32[1,16,8,1024]{3,2,0,1:T(8,128)}), f32[1,16,8,1024]{3,2,0,1:T(8,128)S(1)}, u32[]{:S(2)}, u32[]{:S(2)}) async-start(f32[1,16,8,1024]{3,2,0,1:T(8,128)} %maximum_bitcast_fusion), calls=%async_computation | async-start | bytes 1048576 | tf_op jit(solution)/shard_map/all_to_all | solution.py:161
  10.8 1.3 copy-start.1
  26.6 4.3 %copy-start.2 = (f32[32]{0:T(128)S(1)}, f32[32]{0:T(128)}, u32[]{:S(2)}) copy-start(f32[32]{0:T(128)} %param.11) | copy-start | bytes 388
  26.6 63.5 %all-to-all-start.1 = ((f32[16,6,8,1024]{3,2,1,0:T(8,128)}), f32[16,6,8,1024]{3,2,1,0:T(8,128)S(1)}, u32[]{:S(2)}, u32[]{:S(2)}) async-start(f32[16,6,8,1024]{3,2,1,0:T(8,128)} %bitcast.51), calls=%async_computation.1 | async-start | bytes 6291456 | tf_op jit(solution)/shard_map/all_to_all | solution.py:166
  124.8 74.7 %all-to-all-start.2 = ((f32[6,16,8,1024]{3,2,0,1:T(8,128)}), f32[6,16,8,1024]{3,2,0,1:T(8,128)S(1)}, u32[]{:S(2)}, u32[]{:S(2)}) async-start(f32[6,16,8,1024]{3,2,0,1:T(8,128)} %copy.23), calls=%async_computation.2 | async-start | bytes 6291456 | tf_op jit(solution)/shard_map/all_to_all | solution.py:176
where the time goes:
time: 234 us; the launch traced here: 233 us
  waiting for transfers between devices  130 us (56%)
  blocking collectives  29.5 us (13%)
  Pallas kernels  27.7 us (12%)
  starting transfers between devices  27.1 us (12%)
  local copies, waits for them, and re-layouts  10.3 us (4%)
  other arithmetic  5 us (2%)
  matrix products  2.89 us (1%)
    all_to_all x1, waiting for transfers between devices, local(): lax.all_to_all(spread[wanted], 'seq', split_axis=0, concat_axis=2, tiled=...  59.2 us
    all_to_all x1, waiting for transfers between devices, local(): lax.all_to_all(gradients.reshape(list_len, devices, piece_len, channels),...  58.9 us
    all_to_all x1, blocking collectives, local(): lax.all_to_all(summed.reshape(devices, blocks_here, piece_len, channels),...  29.5 us
    pallas_call x1, Pallas kernels, attend(): pl.pallas_call(attend_kernel, grid=(key_heads, steps), in_specs=[big, big...  27.7 us
    all_to_all x1, starting transfers between devices, local(): lax.all_to_all(gradients.reshape(list_len, devices, piece_len, channels),...  15.4 us
    all_to_all x1, waiting for transfers between devices, local(): lax.all_to_all(stacked, 'seq', split_axis=1, concat_axis=0, tiled=True)  11.9 us
    all_to_all x1, starting transfers between devices, local(): lax.all_to_all(stacked, 'seq', split_axis=1, concat_axis=0, tiled=True)  7.39 us
  transfers between devices with their start and end apart: 3, of which 3 were waited for; matrix products, arithmetic and copies ran while one was open for 1% of the time, Pallas kernels for 0%

commit v1 on v0

--- a/solution.py
+++ b/solution.py
@@ -138,6 +138,437 @@
     return jnp.repeat(jnp.tanh(query_head_gate), D)[None, :]
 
 
+def fused_kernel(
+    devices,
+    k_ref,
+    v_ref,
+    gate_ref,
+    lists_ref,
+    place_ref,
+    q_hbm,
+    g_hbm,
+    out_hbm,
+    gq_hbm,
+    gk_ref,
+    gv_ref,
+    cut,
+    spread0,
+    spread1,
+    spread2,
+    spread3,
+    gathered,
+    grads,
+    sum1,
+    sum2,
+    recv3,
+    back_out,
+    back_in,
+    q_buf,
+    g_buf,
+    out_buf,
+    gq_buf,
+    kcat,
+    vcat,
+    kt2,
+    vt2,
+    in_sem,
+    out_sem,
+    spread_send,
+    spread_recv,
+    z_send,
+    z_recv,
+    x_send,
+    x_recv,
+    s_send,
+    s_recv,
+    r1_send,
+    r1_recv,
+    r2_send,
+    r2_recv,
+    r3_send,
+    r3_recv,
+    back_send,
+    back_recv,
+):
+    spread = (spread0, spread1, spread2, spread3)
+    me = lax.axis_index("seq")
+    c = lax.rem(me, 2)
+    x = lax.rem(me // 2, 2)
+    z = me // 4
+    nz = devices // 4
+    heads = k_ref.shape[1] // D
+    piece = k_ref.shape[0] // devices
+    listed = lists_ref.shape[1]
+    keys = listed * BLOCK_TOKENS
+    rows, width = q_buf.shape
+    wide = HEADS_PER_STEP * D
+    steps = width // heads // wide
+    others = range(1, devices)
+    along_z = range(1, nz)
+
+    def device_at(z, x, c):
+        return {"seq": (z * 2 + x) * 2 + c}
+
+    def remote(src, dst, send, recv, device):
+        return pltpu.make_async_remote_copy(
+            src_ref=src,
+            dst_ref=dst,
+            send_sem=send,
+            recv_sem=recv,
+            device_id=device,
+            device_id_type=MESH,
+        )
+
+    sibling = device_at(z, x, 1 - c)
+    across = device_at(z, 1 - x, c)
+
+    def load_copies(h):
+        part = pl.ds(h * steps * wide, steps * wide)
+        return [
+            pltpu.make_async_copy(q_hbm.at[:, part], q_buf.at[:, part], in_sem.at[0, h]),
+            pltpu.make_async_copy(g_hbm.at[:, part], g_buf.at[:, part], in_sem.at[1, h]),
+        ]
+
+    def store_copies(t):
+        part = pl.ds(pl.multiple_of(t * wide, wide), wide)
+        return [
+            pltpu.make_async_copy(out_buf.at[:, part], out_hbm.at[:, part], out_sem.at[0, t]),
+            pltpu.make_async_copy(gq_buf.at[:, part], gq_hbm.at[:, part], out_sem.at[1, t]),
+        ]
+
+    def spread_copies(h):
+        copies = []
+        for o in others:
+            target = lax.rem(me + o, devices)
+            copies.append(
+                remote(
+                    cut.at[h, target],
+                    spread[h].at[me],
+                    spread_send.at[h, o - 1],
+                    spread_recv.at[h, o - 1],
+                    {"seq": target},
+                )
+            )
+        return copies
+
+    def z_copies(h):
+        own = gathered.at[h, c, x, z]
+        return [
+            remote(
+                own,
+                own,
+                z_send.at[h, o - 1],
+                z_recv.at[h, o - 1],
+                device_at(lax.rem(z + o, nz), x, c),
+            )
+            for o in along_z
+        ]
+
+    def x_copies(h):
+        half = gathered.at[h, c, x]
+        return [remote(half, half, x_send.at[h], x_recv.at[h], across)]
+
+    def s1_copies(h):
+        half = gathered.at[h, c, x]
+        return [remote(half, half, s_send.at[h, 0], s_recv.at[h, 0], sibling)]
+
+    def s2_copies(h):
+        half = gathered.at[h, c, 1 - x]
+        return [remote(half, half, s_send.at[h, 1], s_recv.at[h, 1], sibling)]
+
+    def r1_copies(h):
+        return [remote(grads.at[h, 1 - c], sum1.at[h], r1_send.at[h], r1_recv.at[h], sibling)]
+
+    def r2_copies(h):
+        return [remote(sum1.at[h, 1 - x], sum2.at[h], r2_send.at[h], r2_recv.at[h], across)]
+
+    def r3_copies(h):
+        copies = []
+        for o in along_z:
+            target = lax.rem(z + o, nz)
+            copies.append(
+                remote(
+                    sum2.at[h, target],
+                    recv3.at[h, o - 1],
+                    r3_send.at[h, o - 1],
+                    r3_recv.at[h, o - 1],
+                    device_at(target, x, c),
+                )
+            )
+        return copies
+
+    def back_copies(h):
+        copies = []
+        for o in others:
+            target = lax.rem(me + o, devices)
+            copies.append(
+                remote(
+                    back_out.at[h, target],
+                    back_in.at[h, me],
+                    back_send.at[h, o - 1],
+                    back_recv.at[h, o - 1],
+                    {"seq": target},
+                )
+            )
+        return copies
+
+    def start(copies):
+        for copy in copies:
+            copy.start()
+
+    def arrive(copies):
+        for copy in copies:
+            copy.wait_recv()
+
+    def wanted():
+        return [place_ref[0, lists_ref[0, j]] for j in range(listed)]
+
+    def select_and_send(h):
+        arrive(spread_copies(h))
+        for j, place in enumerate(wanted()):
+            gathered[h, c, x, z, j * piece : (j + 1) * piece, :] = spread[h][place]
+        start(z_copies(h))
+
+    def forward_x(h):
+        arrive(z_copies(h))
+        start(x_copies(h))
+        start(s1_copies(h))
+
+    def forward_s(h):
+        arrive(x_copies(h))
+        start(s2_copies(h))
+
+    def arrived(h):
+        arrive(s1_copies(h))
+        arrive(s2_copies(h))
+
+    def reduce1(h):
+        start(r1_copies(h))
+
+    def reduce2(h):
+        arrive(r1_copies(h))
+        sum1[h] = sum1[h] + grads[h, c]
+        start(r2_copies(h))
+
+    def reduce3(h):
+        arrive(r2_copies(h))
+        sum2[h] = sum2[h] + sum1[h, x]
+        start(r3_copies(h))
+
+    def give_back(h):
+        arrive(r3_copies(h))
+        total = sum2[h, z]
+        for o in along_z:
+            total = total + recv3[h, o - 1]
+        places = wanted()
+        for d in range(devices):
+            held = jnp.zeros((piece, 2 * D), jnp.float32)
+            for j in range(listed):
+                row = total[j * piece : (j + 1) * piece]
+                held = jnp.where(jnp.full(held.shape, places[j]) == d, row, held)
+            back_out[h, d] = held
+        back_in[h, me] = back_out[h, me]
+        start(back_copies(h))
+
+    for h in range(heads):
+        start(load_copies(h))
+    barrier = pltpu.get_barrier_semaphore()
+    for o in others:
+        pl.semaphore_signal(
+            barrier,
+            inc=1,
+            device_id={"seq": lax.rem(me + o, devices)},
+            device_id_type=MESH,
+        )
+    for h in range(heads):
+        part = slice(h * D, (h + 1) * D)
+        both = jnp.concatenate([k_ref[:, part], v_ref[:, part]], axis=1)
+        cut[h] = both.reshape(devices, piece, 2 * D)
+        spread[h][me] = cut[h, me]
+    pl.semaphore_wait(barrier, devices - 1)
+
+    actions = {t: [] for t in range(-1, heads * steps)}
+
+    def at(t, call, h):
+        actions[min(t, heads * steps - 1)].append((call, h))
+
+    last = heads - 1
+    start(spread_copies(0))
+    start(spread_copies(1))
+    select_and_send(0)
+    start(spread_copies(2))
+    forward_x(0)
+    select_and_send(1)
+    start(spread_copies(3))
+    forward_s(0)
+    forward_x(1)
+    arrived(0)
+
+    at(0, forward_s, 1)
+    at(0, select_and_send, 2)
+    at(1, arrived, 1)
+    at(1, forward_x, 2)
+    at(1, select_and_send, 3)
+    at(2, forward_s, 2)
+    at(2, forward_x, 3)
+    at(3, arrived, 2)
+    at(3, forward_s, 3)
+    at(5, arrived, 3)
+    for h in range(heads):
+        end = (h + 1) * steps - 1
+        if h > 0:
+            at(end, reduce3, h - 1)
+        at(end, reduce1, h)
+        if h > 0:
+            at(end + 1, give_back, h - 1)
+        at(end + 1, reduce2, h)
+    at(heads * steps, reduce3, last)
+    at(heads * steps, give_back, last)
+
+    def step(t, carry):
+        h = t // steps
+        s = lax.rem(t, steps)
+
+        @pl.when(s == 0)
+        def _():
+            both = gathered[h].reshape(keys, 2 * D)
+            load_head(both[:, :D], both[:, D:], kcat, vcat, kt2, vt2)
+            for copy in load_copies(h):
+                copy.wait()
+
+        part = pl.ds(pl.multiple_of(t * wide, wide), wide)
+        gate = jnp.concatenate(
+            [
+                jnp.tanh(jnp.full((1, D), gate_ref[0, t * HEADS_PER_STEP + i], jnp.float32))
+                for i in range(HEADS_PER_STEP)
+            ],
+            axis=1,
+        )
+        out, gq, gk, gv = attend_step(
+            q_buf[:, part], g_buf[:, part], gate, kcat, vcat, kt2, vt2
+        )
+        out_buf[:, part] = out
+        gq_buf[:, part] = gq
+        start(store_copies(t))
+        both = jnp.concatenate([gk, gv], axis=1).reshape(2, 2, nz, listed * piece, 2 * D)
+
+        @pl.when(s == 0)
+        def _():
+            grads[h] = both
+
+        @pl.when(s != 0)
+        def _():
+            grads[h] = grads[h] + both
+
+        for when, calls in actions.items():
+            if calls:
+
+                @pl.when(t == when)
+                def _(calls=calls):
+                    for call, head in calls:
+                        call(head)
+
+        return carry
+
+    lax.fori_loop(0, heads * steps, step, 0)
+
+    for h in range(heads):
+        arrive(back_copies(h))
+        part = slice(h * D, (h + 1) * D)
+        both = back_in[h].reshape(devices * piece, 2 * D)
+        gk_ref[:, part] = both[:, :D]
+        gv_ref[:, part] = both[:, D:]
+    for h in range(heads):
+        for make in (
+            spread_copies,
+            z_copies,
+            x_copies,
+            s1_copies,
+            s2_copies,
+            r1_copies,
+            r2_copies,
+            r3_copies,
+            back_copies,
+        ):
+            for copy in make(h):
+                copy.wait_send()
+    for t in range(heads * steps):
+        for copy in store_copies(t):
+            copy.wait()
+
+
+def fused(q, g, k, v, gate, lists, place):
+    devices = lax.axis_size("seq")
+    rows, width = q.shape
+    heads = k.shape[1] // D
+    listed = lists.shape[1]
+    piece = k.shape[0] // devices
+    nz = devices // 4
+    keys = listed * BLOCK_TOKENS
+    total_steps = width // (HEADS_PER_STEP * D)
+    f32 = jnp.float32
+    dma = pltpu.SemaphoreType.DMA
+    vmem = pl.BlockSpec(memory_space=pltpu.VMEM)
+    smem = pl.BlockSpec(memory_space=pltpu.SMEM)
+    hbm = pl.BlockSpec(memory_space=pl.ANY)
+    spread_shape = (heads, devices, piece, 2 * D)
+    per_piece = (listed * piece, 2 * D)
+    return pl.pallas_call(
+        functools.partial(fused_kernel, devices),
+        in_specs=[vmem, vmem, smem, smem, smem, hbm, hbm],
+        out_specs=[hbm, hbm, vmem, vmem],
+        out_shape=[
+            jax.ShapeDtypeStruct(q.shape, f32),
+            jax.ShapeDtypeStruct(q.shape, f32),
+            jax.ShapeDtypeStruct(k.shape, f32),
+            jax.ShapeDtypeStruct(k.shape, f32),
+        ],
+        scratch_shapes=[
+            pltpu.VMEM(spread_shape, f32),
+            pltpu.VMEM(spread_shape[1:], f32),
+            pltpu.VMEM(spread_shape[1:], f32),
+            pltpu.VMEM(spread_shape[1:], f32),
+            pltpu.VMEM(spread_shape[1:], f32),
+            pltpu.VMEM((heads, 2, 2, nz) + per_piece, f32),
+            pltpu.VMEM((heads, 2, 2, nz) + per_piece, f32),
+            pltpu.VMEM((heads, 2, nz) + per_piece, f32),
+            pltpu.VMEM((heads, nz) + per_piece, f32),
+            pltpu.VMEM((heads, nz - 1) + per_piece, f32),
+            pltpu.VMEM(spread_shape, f32),
+            pltpu.VMEM(spread_shape, f32),
+            pltpu.VMEM((rows, width), f32),
+            pltpu.VMEM((rows, width), f32),
+            pltpu.VMEM((rows, width), f32),
+            pltpu.VMEM((rows, width), f32),
+            pltpu.VMEM((keys, 3 * D), jnp.bfloat16),
+            pltpu.VMEM((keys, 3 * D), jnp.bfloat16),
+            pltpu.VMEM((2 * D, keys), jnp.bfloat16),
+            pltpu.VMEM((2 * D, keys), jnp.bfloat16),
+            dma((2, heads)),
+            dma((2, total_steps)),
+            dma((heads, devices - 1)),
+            dma((heads, devices - 1)),
+            dma((heads, nz - 1)),
+            dma((heads, nz - 1)),
+            dma((heads,)),
+            dma((heads,)),
+            dma((heads, 2)),
+            dma((heads, 2)),
+            dma((heads,)),
+            dma((heads,)),
+            dma((heads,)),
+            dma((heads,)),
+            dma((heads, nz - 1)),
+            dma((heads, nz - 1)),
+            dma((heads, devices - 1)),
+            dma((heads, devices - 1)),
+        ],
+        compiler_params=pltpu.CompilerParams(
+            collective_id=0, has_side_effects=True, vmem_limit_bytes=60 * 1024 * 1024
+        ),
+    )(k, v, gate[None, :], lists, place[None, :], q, g)
+
+
 def local(
     queries,
     visual_keys,
@@ -156,6 +587,17 @@
     piece_len = BLOCK_TOKENS // devices
     channels = 2 * feature_width
     positions = devices * blocks_here
+    one_window = window_lists.shape[0] == 1 and devices == window_devices and blocks_here == 1
+    if one_window and devices % 4 == 0 and devices > 4 and feature_width == 4 * D:
+        return fused(
+            queries,
+            output_gradient,
+            visual_keys,
+            visual_value_rows,
+            query_head_gate,
+            window_lists,
+            block_place,
+        )
     stacked = jnp.concatenate([visual_keys, visual_value_rows], axis=1)
     stacked = stacked.reshape(blocks_here, devices, piece_len, channels)
     spread = lax.all_to_all(stacked, "seq", split_axis=1, concat_axis=0, tiled=True).reshape(

time: 234 us -> 105 us (0.45)
  waiting for transfers between devices: 130 us -> 0 us
  Pallas kernels: 27.7 us -> 98.7 us
  blocking collectives: 29.5 us -> 0 us
  starting transfers between devices: 27.1 us -> 0 us
  other arithmetic: 5 us -> 0 us
  local copies, waits for them, and re-layouts: 10.3 us -> 6 us
  matrix products: 2.89 us -> 0 us
    all_to_all x3 -> x0, waiting for transfers between devices: 130 us -> none  [the longest x1 59.2 us: local(): lax.all_to_all(spread[wanted], 'seq', split_axis=0, concat_axis=2, tiled=...]
    pallas_call x1, Pallas kernels: 27.7 us -> 98.7 us  [fused(): pl.pallas_call(functools.partial(fused_kernel, devices), in_specs=[vmem,...]
    all_to_all x1 -> x0, blocking collectives: 29.5 us -> none  [local(): lax.all_to_all(summed.reshape(devices, blocks_here, piece_len, channels),...]
    all_to_all x3 -> x0, starting transfers between devices: 27.1 us -> none  [the longest x1 15.4 us: local(): lax.all_to_all(gradients.reshape(list_len, devices, piece_len, channels),...]
    unnamed x6 -> x10, local copies, waits for them, and re-layouts: 0.02 us -> 6 us
    gather x4 -> x0, local copies, waits for them, and re-layouts: 3.76 us -> none  [the longest x1 2.38 us: local(): spread[wanted]]
    dot_general x1 -> x0, matrix products: 2.89 us -> none  [local(): jnp.dot(onehot, collected.reshape(list_len * devices, piece_len * channel...]
    slice x2 -> x0, local copies, waits for them, and re-layouts: 2.76 us -> none  [the longest x1 1.93 us: local(): fetched[:, feature_width:]]
  transfers between devices with their start and end apart: 3 -> 0, of which waited for: 3 -> 0; matrix products, arithmetic and copies ran while one was open for 1% -> 0% of each run, Pallas kernels for 0% -> 0%
where the time goes in v1:
time: 105 us
  Pallas kernels  98.7 us (94%)
  local copies, waits for them, and re-layouts  6 us (6%)
    pallas_call x1, Pallas kernels, fused(): pl.pallas_call(functools.partial(fused_kernel, devices), in_specs=[vmem,...  98.7 us
    unnamed x10, local copies, waits for them, and re-layouts  6 us

profile of v1, /device:TPU:0, one launch (start us, length us, event | category | flops | bytes accessed | tf_op | source)
XLA Modules:
  0.0 105.3 jit_solution(16769774664048543012)
XLA Ops:
  0.6 98.7 %shard_map.102 = (f32[128,4096]{1,0:T(8,128)}, f32[128,4096]{1,0:T(8,128)}, f32[128,512]{1,0:T(8,128)}, f32[128,512]{1,0:T(8,128)}) custom-call(f32[128,512]{1,0:T(8,128)} %k_ref.1, f32[128,512]{1,0:T(8,128)} %v_ref.1, f32[1,32]{1,0:T(1,128)} %bitcast.2, s32[1,6]{1,0:T(1,128)} %lists_ref.1, s32[1,16]{1,0:T(1,128)} %bitcast.3, f32[128,4096]{1,0:T(8,128)} %q_hbm.1, ...), custom_call_target="tpu_custom_call" | custom-call | tf_op jit(solution)/shard_map/pallas_call | solution.py:516
  99.3 0.0 copy-start
  99.3 3.3 %copy.15 = f32[128,4096]{1,0:T(8,128)} copy(f32[128,4096]{1,0:T(8,128)} %get-tuple-element.8) | data formatting | bytes 4194304
  102.6 0.0 copy-done
  102.6 0.0 copy-start.2
  102.6 0.0 copy-start.1
  102.6 1.3 %copy.16 = f32[128,4096]{1,0:T(8,128)} copy(f32[128,4096]{1,0:T(8,128)S(1)} %copy-done) | data formatting | bytes 4194304
  103.9 0.0 copy-done.2
  103.9 0.7 copy.17
  104.6 0.0 copy-done.1
  104.6 0.7 copy.18
Async XLA Ops:
  99.3 3.3 %copy-start = (f32[128,4096]{1,0:T(8,128)S(1)}, f32[128,4096]{1,0:T(8,128)}, u32[]{:S(2)}) copy-start(f32[128,4096]{1,0:T(8,128)} %get-tuple-element.9) | copy-start | bytes 6291460
  102.6 1.3 %copy-start.2 = (f32[128,512]{1,0:T(8,128)S(1)}, f32[128,512]{1,0:T(8,128)}, u32[]{:S(2)}) copy-start(f32[128,512]{1,0:T(8,128)} %get-tuple-element.10) | copy-start | bytes 786436
  102.6 2.0 %copy-start.1 = (f32[128,512]{1,0:T(8,128)S(1)}, f32[128,512]{1,0:T(8,128)}, u32[]{:S(2)}) copy-start(f32[128,512]{1,0:T(8,128)} %get-tuple-element.11) | copy-start | bytes 786436

commit v2 on v1

--- a/solution.py
+++ b/solution.py
@@ -265,8 +265,11 @@
         ]
 
     def x_copies(h):
-        half = gathered.at[h, c, x]
-        return [remote(half, half, x_send.at[h], x_recv.at[h], across)]
+        copies = []
+        for o in range(nz):
+            own = gathered.at[h, c, x, lax.rem(z + nz - o, nz)]
+            copies.append(remote(own, own, x_send.at[h, o], x_recv.at[h, o], across))
+        return copies
 
     def s1_copies(h):
         half = gathered.at[h, c, x]
@@ -280,7 +283,19 @@
         return [remote(grads.at[h, 1 - c], sum1.at[h], r1_send.at[h], r1_recv.at[h], sibling)]
 
     def r2_copies(h):
-        return [remote(sum1.at[h, 1 - x], sum2.at[h], r2_send.at[h], r2_recv.at[h], across)]
+        copies = []
+        for o in range(nz):
+            row = lax.rem(z + o, nz)
+            copies.append(
+                remote(
+                    sum1.at[h, 1 - x, row],
+                    sum2.at[h, row],
+                    r2_send.at[h, o],
+                    r2_recv.at[h, o],
+                    across,
+                )
+            )
+        return copies
 
     def r3_copies(h):
         copies = []
@@ -328,10 +343,12 @@
         for j, place in enumerate(wanted()):
             gathered[h, c, x, z, j * piece : (j + 1) * piece, :] = spread[h][place]
         start(z_copies(h))
+        start(x_copies(h)[:1])
 
     def forward_x(h):
-        arrive(z_copies(h))
-        start(x_copies(h))
+        for o in along_z:
+            arrive(z_copies(h)[o - 1 : o])
+            start(x_copies(h)[o : o + 1])
         start(s1_copies(h))
 
     def forward_s(h):
@@ -348,12 +365,16 @@
     def reduce2(h):
         arrive(r1_copies(h))
         sum1[h] = sum1[h] + grads[h, c]
-        start(r2_copies(h))
+        copies = r2_copies(h)
+        start(copies[1:] + copies[:1])
 
     def reduce3(h):
-        arrive(r2_copies(h))
-        sum2[h] = sum2[h] + sum1[h, x]
-        start(r3_copies(h))
+        for o in [*along_z, 0]:
+            row = lax.rem(z + o, nz)
+            arrive(r2_copies(h)[o : o + 1])
+            sum2[h, row] = sum2[h, row] + sum1[h, x, row]
+            if o:
+                start(r3_copies(h)[o - 1 : o])
 
     def give_back(h):
         arrive(r3_copies(h))
@@ -397,33 +418,39 @@
     start(spread_copies(1))
     select_and_send(0)
     start(spread_copies(2))
-    forward_x(0)
     select_and_send(1)
     start(spread_copies(3))
+    forward_x(0)
+    select_and_send(2)
     forward_s(0)
     forward_x(1)
     arrived(0)
 
+    at(0, select_and_send, 3)
     at(0, forward_s, 1)
-    at(0, select_and_send, 2)
+    at(1, reduce1, 0)
+    at(1, forward_x, 2)
     at(1, arrived, 1)
-    at(1, forward_x, 2)
-    at(1, select_and_send, 3)
+    at(2, forward_x, 3)
     at(2, forward_s, 2)
-    at(2, forward_x, 3)
+    at(2, reduce2, 0)
+    at(3, reduce1, 1)
     at(3, arrived, 2)
-    at(3, forward_s, 3)
+    at(4, forward_s, 3)
+    at(4, reduce2, 1)
+    at(4, reduce3, 0)
+    at(5, reduce1, 2)
     at(5, arrived, 3)
-    for h in range(heads):
-        end = (h + 1) * steps - 1
-        if h > 0:
-            at(end, reduce3, h - 1)
-        at(end, reduce1, h)
-        if h > 0:
-            at(end + 1, give_back, h - 1)
-        at(end + 1, reduce2, h)
-    at(heads * steps, reduce3, last)
-    at(heads * steps, give_back, last)
+    at(5, give_back, 0)
+    at(6, reduce2, 2)
+    at(6, reduce3, 1)
+    at(7, reduce1, last)
+    at(7, give_back, 1)
+    at(7, reduce2, last)
+    at(7, reduce3, 2)
+    at(7, reduce3, last)
+    at(7, give_back, 2)
+    at(7, give_back, last)
 
     def step(t, carry):
         h = t // steps
@@ -511,11 +538,12 @@
     vmem = pl.BlockSpec(memory_space=pltpu.VMEM)
     smem = pl.BlockSpec(memory_space=pltpu.SMEM)
     hbm = pl.BlockSpec(memory_space=pl.ANY)
+    far = pl.BlockSpec(memory_space=pltpu.HBM)
     spread_shape = (heads, devices, piece, 2 * D)
     per_piece = (listed * piece, 2 * D)
     return pl.pallas_call(
         functools.partial(fused_kernel, devices),
-        in_specs=[vmem, vmem, smem, smem, smem, hbm, hbm],
+        in_specs=[vmem, vmem, smem, smem, smem, far, far],
         out_specs=[hbm, hbm, vmem, vmem],
         out_shape=[
             jax.ShapeDtypeStruct(q.shape, f32),
@@ -550,14 +578,14 @@
             dma((heads, devices - 1)),
             dma((heads, nz - 1)),
             dma((heads, nz - 1)),
-            dma((heads,)),
-            dma((heads,)),
+            dma((heads, nz)),
+            dma((heads, nz)),
             dma((heads, 2)),
             dma((heads, 2)),
             dma((heads,)),
             dma((heads,)),
-            dma((heads,)),
-            dma((heads,)),
+            dma((heads, nz)),
+            dma((heads, nz)),
             dma((heads, nz - 1)),
             dma((heads, nz - 1)),
             dma((heads, devices - 1)),

time: 105 us -> 91.8 us (0.87)
  Pallas kernels: 98.7 us -> 85 us
    pallas_call x1, Pallas kernels: 98.7 us -> 85 us  [fused(): pl.pallas_call(functools.partial(fused_kernel, devices), in_specs=[vmem,...]
where the time goes in v2:
time: 91.8 us; the launch traced here: 91.7 us
  Pallas kernels  85 us (93%)
  local copies, waits for them, and re-layouts  6 us (7%)
    pallas_call x1, Pallas kernels, fused(): pl.pallas_call(functools.partial(fused_kernel, devices), in_specs=[vmem,...  85 us
    unnamed x10, local copies, waits for them, and re-layouts  6 us

profile of v2, /device:TPU:0, one launch (start us, length us, event | category | flops | bytes accessed | tf_op | source)
XLA Modules:
  0.0 91.7 jit_solution(8278099921485097468)
XLA Ops:
  0.6 85.0 %shard_map.102 = (f32[128,4096]{1,0:T(8,128)}, f32[128,4096]{1,0:T(8,128)}, f32[128,512]{1,0:T(8,128)}, f32[128,512]{1,0:T(8,128)}) custom-call(f32[128,512]{1,0:T(8,128)} %k_ref.1, f32[128,512]{1,0:T(8,128)} %v_ref.1, f32[1,32]{1,0:T(1,128)} %bitcast.2, s32[1,6]{1,0:T(1,128)} %lists_ref.1, s32[1,16]{1,0:T(1,128)} %bitcast.3, f32[128,4096]{1,0:T(8,128)} %q_hbm.1, ...), custom_call_target="tpu_custom_call" | custom-call | tf_op jit(solution)/shard_map/pallas_call | solution.py:544
  85.7 0.0 copy-start
  85.7 3.3 %copy.15 = f32[128,4096]{1,0:T(8,128)} copy(f32[128,4096]{1,0:T(8,128)} %get-tuple-element.8) | data formatting | bytes 4194304
  88.9 0.0 copy-done
  88.9 0.0 copy-start.2
  88.9 0.0 copy-start.1
  88.9 1.3 %copy.16 = f32[128,4096]{1,0:T(8,128)} copy(f32[128,4096]{1,0:T(8,128)S(1)} %copy-done) | data formatting | bytes 4194304
  90.3 0.0 copy-done.2
  90.3 0.7 copy.17
  91.0 0.0 copy-done.1
  91.0 0.7 copy.18
Async XLA Ops:
  85.7 3.3 %copy-start = (f32[128,4096]{1,0:T(8,128)S(1)}, f32[128,4096]{1,0:T(8,128)}, u32[]{:S(2)}) copy-start(f32[128,4096]{1,0:T(8,128)} %get-tuple-element.9) | copy-start | bytes 6291460
  88.9 1.3 %copy-start.2 = (f32[128,512]{1,0:T(8,128)S(1)}, f32[128,512]{1,0:T(8,128)}, u32[]{:S(2)}) copy-start(f32[128,512]{1,0:T(8,128)} %get-tuple-element.10) | copy-start | bytes 786436
  88.9 2.0 %copy-start.1 = (f32[128,512]{1,0:T(8,128)S(1)}, f32[128,512]{1,0:T(8,128)}, u32[]{:S(2)}) copy-start(f32[128,512]{1,0:T(8,128)} %get-tuple-element.11) | copy-start | bytes 786436
